TPU v7x, 32 devices: a whole 2x2x4 slice. The times are simulated.
32 devices in a mesh: groups: 2 (over y), tmpl: 16 (over z, x, core).
Axes of the slice: x: 2, y: 2, z: 4, core: 2. Of those that a mesh axis runs over, the one named last changes fastest.
Arguments:
- records: bfloat16 [512, 3, 768], P(('groups', 'tmpl')), parts along dimension 0, may hold values from -200 to 200, as said below
- templates: bfloat16 [96, 20, 3, 300], P('tmpl'), may hold values from -6 to 6
- fetch_list: int32 [16, 16, 2], P('tmpl'), may hold values from -1 to 15, as said below
- cluster_slots: int32 [96, 20], P('tmpl'), may hold values from 0 to 31, as said below
- moveouts: int32 [96, 20], P('tmpl'), may hold values from 0 to 213
Outputs:
- stack: float32 [192, 256], P(('groups', 'tmpl')), parts along dimension 0
- network_peak: float32 [512], P('groups'), parts along dimension 0
There are 2 independent parts, one for each index of `groups`. A program takes and returns all parts, laid end to end along the dimension named above; an argument that names none is the same for every part. Nothing has to cross between parts.
Inputs may be any that keep to these rules, and one draw needn't show every extreme that they name: Values are the records' samples; the amplitude of a station component is steady apart from one event burst. fetch_list[g, o, s] is an index among holder o's 16 stations, or -1 for an empty slot; the set entries of one (g, o) pair differ; every group g has all 2 slots set for the holders g to g + 20 // 2 - 1 (modulo 16). cluster_slots[k, j] is a slot o * 2 + s of group k // 6 whose fetch_list entry is set; the 20 entries of a station set differ, and every set slot of a group is named by some station set of that group.
All inputs are finite; a program needn't handle non-finite values.
Results may differ from a plain program's by a relative error of at most 0.0003.
Values may be sent and summed in bfloat16 or wider, within the bound.
A program may use at most 64 MiB of HBM per device.

v0:
```python
import jax
import jax.numpy as jnp
from jax import lax
from jax.sharding import PartitionSpec as P

OUT = 256


def batch_stack(traces, kernels, shifts):
    sets_here, stations, comps, rec_len = traces.shape
    members = kernels.shape[1]
    tap_count = kernels.shape[-1]
    lag_count = rec_len - tap_count + 1
    inputs_nch = traces.reshape(1, sets_here * stations * comps, rec_len)
    filters = jnp.transpose(kernels, (0, 2, 3, 1, 4)).reshape(
        sets_here * stations * comps * members, 1, tap_count
    )
    products = lax.conv_general_dilated(
        inputs_nch,
        filters,
        (1,),
        "VALID",
        dimension_numbers=("NCH", "OIH", "NCH"),
        feature_group_count=sets_here * stations * comps,
        preferred_element_type=jnp.float32,
    )[0]
    products = products.reshape(sets_here, stations, comps, members, lag_count)
    widened = traces.astype(jnp.float32)
    running = jnp.cumsum(widened * widened, axis=-1)
    running = jnp.concatenate(
        [jnp.zeros((sets_here, stations, comps, 1), jnp.float32), running], axis=-1
    )
    energy = running[..., tap_count:] - running[..., :lag_count]
    data_scale = jnp.sqrt(energy / tap_count + 1e-05)
    kernels_wide = kernels.astype(jnp.float32)
    tmpl_scale = jnp.sqrt(jnp.mean(kernels_wide * kernels_wide, axis=-1) + 1e-05)
    tmpl_scale = jnp.transpose(tmpl_scale, (0, 2, 3, 1))[..., None]
    normed = products / (tap_count * tmpl_scale * data_scale[:, :, :, None, :])
    channel_sum = jnp.sum(normed, axis=2)
    offsets = jnp.transpose(shifts, (0, 2, 1))[..., None] + jnp.arange(OUT, dtype=jnp.int32)
    aligned = jnp.take_along_axis(channel_sum, offsets, axis=3)
    return jnp.sum(aligned, axis=1)


def on_device(records, templates, fetch_list, cluster_slots, moveouts):
    owners = lax.axis_size("tmpl")
    per_owner = fetch_list.shape[2]
    stations_here = records.shape[0]
    slot_total = owners * per_owner
    wanted = fetch_list.reshape(slot_total)
    block_rows = lax.all_gather(records, "tmpl", axis=0, tiled=True)
    owners_in = block_rows.shape[0] // stations_here
    row_ids = jnp.arange(
        owners_in * per_owner, dtype=jnp.int32
    ) // per_owner * stations_here + jnp.clip(wanted, 0, stations_here - 1)
    rows_taken = jnp.take(block_rows, row_ids, axis=0)
    rows_taken = jnp.where(
        (wanted >= 0)[:, None, None], rows_taken, jnp.zeros((), block_rows.dtype)
    )
    clusters_here = cluster_slots.shape[0]
    members = templates.shape[0] // clusters_here
    kernels_all = templates.reshape((clusters_here, members) + templates.shape[1:])
    shifts_all = moveouts.reshape(clusters_here, members, moveouts.shape[1])
    traces = jnp.take(rows_taken, cluster_slots, axis=0)
    stacks = batch_stack(traces, kernels_all, shifts_all)
    stack = stacks.reshape(clusters_here * members, stacks.shape[-1])
    network_peak = lax.pmax(jnp.max(stack, axis=0), "tmpl")
    return (stack, network_peak)


def solution(mesh):
    placed = (
        P(("groups", "tmpl"), None, None),
        P("tmpl", None, None, None),
        P("tmpl", None, None),
        P("tmpl", None),
        P("tmpl", None),
    )
    return jax.shard_map(
        on_device,
        mesh=mesh,
        in_specs=placed,
        out_specs=(P(("groups", "tmpl"), None), P("groups")),
        check_vma=False,
    )
```

profile of v0, /device:TPU:0, one launch (start us, length us, event | category | flops | bytes accessed | tf_op | source)
XLA Modules:
  0.0 464.8 jit_solution(15089831089222544754)
XLA Ops:
  7.2 0.7 all-gather.2.cloned.1.call-update
  7.9 0.7 broadcast_clamp_fusion
  8.9 0.7 broadcast_compare_fusion
  9.8 0.7 compare_select_fusion.2
  10.5 0.7 compare_and_fusion
  11.5 1.1 copy.62
  12.9 1.3 copy.64
  14.8 36.6 %all-gather.2.cloned.1.call-done = bf16[256,3,768]{2,0,1:T(8,128)(2,1)} async-done(((bf16[16,3,768]{2,0,1:T(8,128)(2,1)}), bf16[256,3,768]{2,0,1:T(8,128)(2,1)}) %all-gather.2.cloned.1.call-update) | async-done | bytes 1179664 | tf_op jit(solution)/shard_map/all_gather | solution.py:51
  51.4 2.3 copy.61
  53.7 0.7 gather_fusion
  54.6 1.2 gather_fusion.1
  55.8 0.5 reshape.256
  56.4 1.3 gather.18
  57.9 30.9 %reduce-window.6 = f32[6,20,3,6,128]{4,1,2,3,0:T(8,128)S(1)} reduce-window(f32[6,20,3,6,128]{4,1,2,3,0:T(8,128)S(1)} %copy.70, f32[]{:T(128)} %constant.84.clone.1), window={size=1x1x1x1x128 pad=0_0x0_0x0_0x0_0x127_0}, to_apply=%region_1.2 | reduce-window | flops 35112960 | bytes 2211844 | tf_op jit(solution)/shard_map/reduce-window
  89.3 1.0 copy.71
  90.4 0.5 broadcast_add_fusion
  91.1 0.6 reshape.257
  91.7 1.2 broadcast_select_fusion
  92.8 1.3 copy.63
  94.2 25.0 %fusion.19 = f32[1,360,469]{1,0,2:T(1,128)} fusion(bf16[1,360,768]{1,0,2:T(2,128)(2,1)S(1)} %copy.63, bf16[360,1,300]{0,1,2:T(2,128)(2,1)} %copy.64), kind=kOutput, calls=%fused_computation.50 | convolution fusion | flops 101304000 | bytes 1444320 | tf_op jit(solution)/shard_map/conv_general_dilated | solution.py:18
  119.1 2.3 copy.65
  121.8 2.3 fusion.6
  124.1 301.2 %gather_fusion.2 = f32[30720]{0:T(1024)S(1)} fusion(f32[6,20,469]{2,1,0:T(8,128)S(1)} %fusion.6, s32[30720]{0:T(1024)S(1)} %reshape.244), kind=kCustom, calls=%fused_computation.2 | custom fusion | bytes 614400 | tf_op jit(solution)/shard_map/jit(take_along_axis)/gather | solution.py:41
  425.7 32.2 %pmax.7 = f32[256]{0:T(256)} all-reduce(f32[256]{0:T(256)S(1)} %reduce_max.9), channel_id=1, replica_groups=mesh['groups'=2,'tmpl'=16] {'tmpl'}, use_global_device_ids=true, to_apply=%region_6.7 | all-reduce | flops 256 | bytes 2048 | tf_op jit(solution)/shard_map/pmax | solution.py:67
  (35 shorter events, 3.6 us)
Async XLA Ops:
  7.2 7.1 %copy-start = (bf16[6,20,3,300]{3,1,2,0:T(8,128)(2,1)S(1)}, bf16[6,20,3,300]{3,1,2,0:T(8,128)(2,1)}, u32[]{:S(2)}) copy-start(bf16[6,20,3,300]{3,1,2,0:T(8,128)(2,1)} %param.6) | copy-start | bytes 648004
  7.2 7.4 %copy-start.2 = (s32[6,20]{1,0:T(8,128)S(1)}, s32[6,20]{1,0:T(8,128)}, u32[]{:S(2)}) copy-start(s32[6,20]{1,0:T(8,128)} %param.9) | copy-start | bytes 1444
  7.2 44.2 %all-gather.2.cloned.1.call-start = ((), (), s32[]{:S(2)}) async-start(), calls=%async_computation | async-start | bytes 1253376 | tf_op jit(solution)/shard_map/all_gather | solution.py:51
  425.7 32.2 %copy-start.1 = (f32[6,256]{1,0:T(8,128)}, f32[6,256]{1,0:T(8,128)S(1)}, u32[]{:S(2)}) copy-start(f32[6,256]{1,0:T(8,128)S(1)} %fusion.10) | copy-start | bytes 18436
Sparse Core Ops, SparseCore 0:
  10.3 41.0 all-gather.1
where the time goes:
time: 465 us
  local copies, waits for them, and re-layouts  317 us (68%)
  other arithmetic  38.9 us (8%)
  waiting for transfers between devices  37.3 us (8%)
  blocking collectives  32.2 us (7%)
  matrix products  25 us (5%)
  between operations  14.3 us (3%)
    gather x2, local copies, waits for them, and re-layouts, batch_stack(): aligned = jnp.take_along_axis(channel_sum, offsets, axis=3)  301 us
    all_gather x1, waiting for transfers between devices, on_device(): block_rows = lax.all_gather(records, 'tmpl', axis=0, tiled=True)  36.6 us
    pmax x1, blocking collectives, on_device(): network_peak = lax.pmax(jnp.max(stack, axis=0), 'tmpl')  32.2 us
    another operation x3, other arithmetic  31.5 us
    conv_general_dilated x1, matrix products, batch_stack(): lax.conv_general_dilated(inputs_nch, filters, (1,), 'VALID', dimension_nu...  25 us
  transfers between devices with their start and end apart: 1, of which 1 were waited for; matrix products, arithmetic and copies ran while one was open for 1% of the time, Pallas kernels for 0%

commit v1 on v0

--- a/solution.py
+++ b/solution.py
@@ -1,9 +1,30 @@
+import functools
 import jax
 import jax.numpy as jnp
 from jax import lax
 from jax.sharding import PartitionSpec as P
 
 OUT = 256
+
+
+def _rest_tasks(v0, axis_id):
+    world_n = jax.lax.axis_size(axis_id)
+    t1 = range(1, world_n)
+    local_out = list(map(lambda c: (c - 1, c), t1))
+    answer = local_out + [(world_n - 1, 0)]
+    u1 = v0
+    row_list = [u1]
+    h = 0
+    while h < world_n - 1:
+        u1 = jax.lax.ppermute(u1, axis_id, answer)
+        row_list += [u1]
+        h = h + 1
+    upper = jnp.concatenate([*reversed(row_list)], axis=0)
+    back = jnp.roll(upper, (jax.lax.axis_index(axis_id) + 1) * u1.shape[0], 0)
+    return back
+
+
+point_digits_up = functools.partial(_rest_tasks, axis_id="tmpl")
 
 
 def batch_stack(traces, kernels, shifts):
@@ -48,7 +69,7 @@
     stations_here = records.shape[0]
     slot_total = owners * per_owner
     wanted = fetch_list.reshape(slot_total)
-    block_rows = lax.all_gather(records, "tmpl", axis=0, tiled=True)
+    block_rows = point_digits_up(records)
     owners_in = block_rows.shape[0] // stations_here
     row_ids = jnp.arange(
         owners_in * per_owner, dtype=jnp.int32

time: 465 us -> 509 us (1.095)
  waiting for transfers between devices: 37.3 us -> 93.1 us
  between operations: 14.3 us -> 1.07 us
    ppermute x0 -> x15, waiting for transfers between devices: none -> 93.1 us  [_rest_tasks(): u1 = jax.lax.ppermute(u1, axis_id, answer)]
    all_gather x1 -> x0, waiting for transfers between devices: 36.6 us -> none  [on_device(): block_rows = lax.all_gather(records, 'tmpl', axis=0, tiled=True)]
  transfers between devices with their start and end apart: 1 -> 15, of which waited for: 1 -> 15; matrix products, arithmetic and copies ran while one was open for 1% -> 2% of each run, Pallas kernels for 0% -> 0%
where the time goes in v1:
time: 509 us; the launch traced here: 508 us
  local copies, waits for them, and re-layouts  318 us (62%)
  waiting for transfers between devices  93.1 us (18%)
  other arithmetic  40.4 us (8%)
  blocking collectives  30 us (6%)
  matrix products  24.8 us (5%)
    gather x2, local copies, waits for them, and re-layouts, batch_stack(): aligned = jnp.take_along_axis(channel_sum, offsets, axis=3)  301 us
    ppermute x15, waiting for transfers between devices, _rest_tasks(): u1 = jax.lax.ppermute(u1, axis_id, answer)  93.1 us
    another operation x3, other arithmetic  31.4 us
    pmax x1, blocking collectives, on_device(): network_peak = lax.pmax(jnp.max(stack, axis=0), 'tmpl')  30 us
    conv_general_dilated x1, matrix products, batch_stack(): lax.conv_general_dilated(inputs_nch, filters, (1,), 'VALID', dimension_nu...  24.8 us
  transfers between devices with their start and end apart: 15, of which 15 were waited for; matrix products, arithmetic and copies ran while one was open for 2% of the time, Pallas kernels for 0%

profile of v1, /device:TPU:0, one launch (start us, length us, event | category | flops | bytes accessed | tf_op | source)
XLA Modules:
  0.0 508.3 jit_solution(12030554645026508508)
XLA Ops:
  2.1 7.3 %collective-permute-done = bf16[16,3,768]{2,1,0:T(4,128)(2,1)S(1)} collective-permute-done((bf16[16,3,768]{2,1,0:T(4,128)(2,1)S(1)}, bf16[16,3,768]{2,1,0:T(4,128)(2,1)S(1)}, u32[]{:S(2)}, u32[]{:S(2)}) %collective-permute-start) | collective-permute-done | bytes 73760 | tf_op jit(solution)/shard_map/ppermute | solution.py:19
  9.4 6.7 %collective-permute-done.1 = bf16[16,3,768]{2,1,0:T(4,128)(2,1)S(1)} collective-permute-done((bf16[16,3,768]{2,1,0:T(4,128)(2,1)S(1)}, bf16[16,3,768]{2,1,0:T(4,128)(2,1)S(1)}, u32[]{:S(2)}, u32[]{:S(2)}) %collective-permute-start.1) | collective-permute-done | bytes 73760 | tf_op jit(solution)/shard_map/ppermute | solution.py:19
  16.2 6.7 %collective-permute-done.2 = bf16[16,3,768]{2,1,0:T(4,128)(2,1)S(1)} collective-permute-done((bf16[16,3,768]{2,1,0:T(4,128)(2,1)S(1)}, bf16[16,3,768]{2,1,0:T(4,128)(2,1)S(1)}, u32[]{:S(2)}, u32[]{:S(2)}) %collective-permute-start.2) | collective-permute-done | bytes 73760 | tf_op jit(solution)/shard_map/ppermute | solution.py:19
  22.9 6.7 %collective-permute-done.3 = bf16[16,3,768]{2,1,0:T(4,128)(2,1)S(1)} collective-permute-done((bf16[16,3,768]{2,1,0:T(4,128)(2,1)S(1)}, bf16[16,3,768]{2,1,0:T(4,128)(2,1)S(1)}, u32[]{:S(2)}, u32[]{:S(2)}) %collective-permute-start.3) | collective-permute-done | bytes 73760 | tf_op jit(solution)/shard_map/ppermute | solution.py:19
  29.6 6.7 %collective-permute-done.4 = bf16[16,3,768]{2,1,0:T(4,128)(2,1)S(1)} collective-permute-done((bf16[16,3,768]{2,1,0:T(4,128)(2,1)S(1)}, bf16[16,3,768]{2,1,0:T(4,128)(2,1)S(1)}, u32[]{:S(2)}, u32[]{:S(2)}) %collective-permute-start.4) | collective-permute-done | bytes 73760 | tf_op jit(solution)/shard_map/ppermute | solution.py:19
  37.2 5.9 %collective-permute-done.5 = bf16[16,3,768]{2,1,0:T(4,128)(2,1)S(1)} collective-permute-done((bf16[16,3,768]{2,1,0:T(4,128)(2,1)S(1)}, bf16[16,3,768]{2,1,0:T(4,128)(2,1)S(1)}, u32[]{:S(2)}, u32[]{:S(2)}) %collective-permute-start.5) | collective-permute-done | bytes 73760 | tf_op jit(solution)/shard_map/ppermute | solution.py:19
  44.2 5.6 %collective-permute-done.6 = bf16[16,3,768]{2,1,0:T(4,128)(2,1)S(1)} collective-permute-done((bf16[16,3,768]{2,1,0:T(4,128)(2,1)S(1)}, bf16[16,3,768]{2,1,0:T(4,128)(2,1)S(1)}, u32[]{:S(2)}, u32[]{:S(2)}) %collective-permute-start.6) | collective-permute-done | bytes 73760 | tf_op jit(solution)/shard_map/ppermute | solution.py:19
  49.9 6.7 %collective-permute-done.7 = bf16[16,3,768]{2,1,0:T(4,128)(2,1)S(1)} collective-permute-done((bf16[16,3,768]{2,1,0:T(4,128)(2,1)S(1)}, bf16[16,3,768]{2,1,0:T(4,128)(2,1)S(1)}, u32[]{:S(2)}, u32[]{:S(2)}) %collective-permute-start.7) | collective-permute-done | bytes 73760 | tf_op jit(solution)/shard_map/ppermute | solution.py:19
  57.3 6.0 %collective-permute-done.8 = bf16[16,3,768]{2,1,0:T(4,128)(2,1)S(1)} collective-permute-done((bf16[16,3,768]{2,1,0:T(4,128)(2,1)S(1)}, bf16[16,3,768]{2,1,0:T(4,128)(2,1)S(1)}, u32[]{:S(2)}, u32[]{:S(2)}) %collective-permute-start.8) | collective-permute-done | bytes 73760 | tf_op jit(solution)/shard_map/ppermute | solution.py:19
  64.0 6.0 %collective-permute-done.9 = bf16[16,3,768]{2,1,0:T(4,128)(2,1)S(1)} collective-permute-done((bf16[16,3,768]{2,1,0:T(4,128)(2,1)S(1)}, bf16[16,3,768]{2,1,0:T(4,128)(2,1)S(1)}, u32[]{:S(2)}, u32[]{:S(2)}) %collective-permute-start.9) | collective-permute-done | bytes 73760 | tf_op jit(solution)/shard_map/ppermute | solution.py:19
  70.8 6.1 %collective-permute-done.10 = bf16[16,3,768]{2,1,0:T(4,128)(2,1)S(1)} collective-permute-done((bf16[16,3,768]{2,1,0:T(4,128)(2,1)S(1)}, bf16[16,3,768]{2,1,0:T(4,128)(2,1)S(1)}, u32[]{:S(2)}, u32[]{:S(2)}) %collective-permute-start.10) | collective-permute-done | bytes 73760 | tf_op jit(solution)/shard_map/ppermute | solution.py:19
  77.7 5.9 %collective-permute-done.11 = bf16[16,3,768]{2,1,0:T(4,128)(2,1)S(1)} collective-permute-done((bf16[16,3,768]{2,1,0:T(4,128)(2,1)S(1)}, bf16[16,3,768]{2,1,0:T(4,128)(2,1)S(1)}, u32[]{:S(2)}, u32[]{:S(2)}) %collective-permute-start.11) | collective-permute-done | bytes 73760 | tf_op jit(solution)/shard_map/ppermute | solution.py:19
  83.6 6.6 %collective-permute-done.12 = bf16[16,3,768]{2,1,0:T(4,128)(2,1)S(1)} collective-permute-done((bf16[16,3,768]{2,1,0:T(4,128)(2,1)S(1)}, bf16[16,3,768]{2,1,0:T(4,128)(2,1)S(1)}, u32[]{:S(2)}, u32[]{:S(2)}) %collective-permute-start.12) | collective-permute-done | bytes 73760 | tf_op jit(solution)/shard_map/ppermute | solution.py:19
  92.3 1.3 copy.72
  93.8 3.3 collective-permute-done.13
  97.0 6.7 %collective-permute-done.14 = bf16[16,3,768]{2,1,0:T(4,128)(2,1)S(1)} collective-permute-done((bf16[16,3,768]{2,1,0:T(4,128)(2,1)S(1)}, bf16[16,3,768]{2,1,0:T(4,128)(2,1)S(1)}, u32[]{:S(2)}, u32[]{:S(2)}) %collective-permute-start.14) | collective-permute-done | bytes 73760 | tf_op jit(solution)/shard_map/ppermute | solution.py:19
  109.0 1.3 gather.18
  110.5 30.9 %reduce-window.6 = f32[6,20,3,6,128]{4,1,2,3,0:T(8,128)S(1)} reduce-window(f32[6,20,3,6,128]{4,1,2,3,0:T(8,128)S(1)} %copy.78, f32[]{:T(128)} %constant.109.clone.1), window={size=1x1x1x1x128 pad=0_0x0_0x0_0x0_0x127_0}, to_apply=%region_1.2 | reduce-window | flops 35112960 | bytes 2211844 | tf_op jit(solution)/shard_map/reduce-window
  145.4 1.3 copy.71
  146.7 24.8 %fusion.19 = f32[1,360,469]{1,0,2:T(1,128)} fusion(bf16[1,360,768]{1,0,2:T(2,128)(2,1)S(1)} %copy.71, bf16[360,1,300]{0,1,2:T(2,128)(2,1)} %copy.72), kind=kOutput, calls=%fused_computation.83 | convolution fusion | flops 101304000 | bytes 1444320 | tf_op jit(solution)/shard_map/conv_general_dilated | solution.py:39
  171.5 2.5 copy.73
  174.4 2.3 fusion.6
  176.6 301.2 %gather_fusion.2 = f32[30720]{0:T(1024)S(1)} fusion(f32[6,20,469]{2,1,0:T(8,128)S(1)} %fusion.6, s32[30720]{0:T(1024)S(1)} %reshape.244), kind=kCustom, calls=%fused_computation.2 | custom fusion | bytes 614400 | tf_op jit(solution)/shard_map/jit(take_along_axis)/gather | solution.py:62
  478.2 30.0 %pmax.7 = f32[256]{0:T(256)} all-reduce(f32[256]{0:T(256)S(1)} %reduce_max.9), channel_id=1, replica_groups=mesh['groups'=2,'tmpl'=16] {'tmpl'}, use_global_device_ids=true, to_apply=%region_6.7 | all-reduce | flops 256 | bytes 2048 | tf_op jit(solution)/shard_map/pmax | solution.py:88
  (94 shorter events, 18.5 us)
Async XLA Ops:
  0.6 103.9 %copy-start = (bf16[16,3,768]{2,0,1:T(8,128)(2,1)S(1)}, bf16[16,3,768]{2,0,1:T(8,128)(2,1)}, u32[]{:S(2)}) copy-start(bf16[16,3,768]{2,0,1:T(8,128)(2,1)} %param.5) | copy-start | bytes 221188
  1.6 7.8 %collective-permute-start = (bf16[16,3,768]{2,1,0:T(4,128)(2,1)S(1)}, bf16[16,3,768]{2,1,0:T(4,128)(2,1)S(1)}, u32[]{:S(2)}, u32[]{:S(2)}) collective-permute-start(bf16[16,3,768]{2,1,0:T(4,128)(2,1)S(1)} %copy.66), channel_id=1, source_target_pairs={{0,1},{1,2},{2,3},{3,4},{4,5},{5,6},{6,7},{7,8},{8,9},{9,10},{10,1... | collective-permute-start | bytes 221192 | tf_op jit(solution)/shard_map/ppermute | solution.py:19
  9.4 6.7 %collective-permute-start.1 = (bf16[16,3,768]{2,1,0:T(4,128)(2,1)S(1)}, bf16[16,3,768]{2,1,0:T(4,128)(2,1)S(1)}, u32[]{:S(2)}, u32[]{:S(2)}) collective-permute-start(bf16[16,3,768]{2,1,0:T(4,128)(2,1)S(1)} %collective-permute-done), channel_id=1, source_target_pairs={{0,1},{1,2},{2,3},{3,4},{4,5},{5,6},{6,7},{7,8},{8,9},{9,10},{10,1... | collective-permute-start | bytes 221192 | tf_op jit(solution)/shard_map/ppermute | solution.py:19
  16.2 6.7 %collective-permute-start.2 = (bf16[16,3,768]{2,1,0:T(4,128)(2,1)S(1)}, bf16[16,3,768]{2,1,0:T(4,128)(2,1)S(1)}, u32[]{:S(2)}, u32[]{:S(2)}) collective-permute-start(bf16[16,3,768]{2,1,0:T(4,128)(2,1)S(1)} %collective-permute-done.1), channel_id=1, source_target_pairs={{0,1},{1,2},{2,3},{3,4},{4,5},{5,6},{6,7},{7,8},{8,9},{9,10},{10,1... | collective-permute-start | bytes 221192 | tf_op jit(solution)/shard_map/ppermute | solution.py:19
  22.9 6.7 %collective-permute-start.3 = (bf16[16,3,768]{2,1,0:T(4,128)(2,1)S(1)}, bf16[16,3,768]{2,1,0:T(4,128)(2,1)S(1)}, u32[]{:S(2)}, u32[]{:S(2)}) collective-permute-start(bf16[16,3,768]{2,1,0:T(4,128)(2,1)S(1)} %collective-permute-done.2), channel_id=1, source_target_pairs={{0,1},{1,2},{2,3},{3,4},{4,5},{5,6},{6,7},{7,8},{8,9},{9,10},{10,1... | collective-permute-start | bytes 221192 | tf_op jit(solution)/shard_map/ppermute | solution.py:19
  29.6 6.7 %collective-permute-start.4 = (bf16[16,3,768]{2,1,0:T(4,128)(2,1)S(1)}, bf16[16,3,768]{2,1,0:T(4,128)(2,1)S(1)}, u32[]{:S(2)}, u32[]{:S(2)}) collective-permute-start(bf16[16,3,768]{2,1,0:T(4,128)(2,1)S(1)} %collective-permute-done.3), channel_id=1, source_target_pairs={{0,1},{1,2},{2,3},{3,4},{4,5},{5,6},{6,7},{7,8},{8,9},{9,10},{10,1... | collective-permute-start | bytes 221192 | tf_op jit(solution)/shard_map/ppermute | solution.py:19
  36.4 6.7 %collective-permute-start.5 = (bf16[16,3,768]{2,1,0:T(4,128)(2,1)S(1)}, bf16[16,3,768]{2,1,0:T(4,128)(2,1)S(1)}, u32[]{:S(2)}, u32[]{:S(2)}) collective-permute-start(bf16[16,3,768]{2,1,0:T(4,128)(2,1)S(1)} %collective-permute-done.4), channel_id=1, source_target_pairs={{0,1},{1,2},{2,3},{3,4},{4,5},{5,6},{6,7},{7,8},{8,9},{9,10},{10,1... | collective-permute-start | bytes 221192 | tf_op jit(solution)/shard_map/ppermute | solution.py:19
  43.1 6.7 %collective-permute-start.6 = (bf16[16,3,768]{2,1,0:T(4,128)(2,1)S(1)}, bf16[16,3,768]{2,1,0:T(4,128)(2,1)S(1)}, u32[]{:S(2)}, u32[]{:S(2)}) collective-permute-start(bf16[16,3,768]{2,1,0:T(4,128)(2,1)S(1)} %collective-permute-done.5), channel_id=1, source_target_pairs={{0,1},{1,2},{2,3},{3,4},{4,5},{5,6},{6,7},{7,8},{8,9},{9,10},{10,1... | collective-permute-start | bytes 221192 | tf_op jit(solution)/shard_map/ppermute | solution.py:19
  49.8 6.7 %collective-permute-start.7 = (bf16[16,3,768]{2,1,0:T(4,128)(2,1)S(1)}, bf16[16,3,768]{2,1,0:T(4,128)(2,1)S(1)}, u32[]{:S(2)}, u32[]{:S(2)}) collective-permute-start(bf16[16,3,768]{2,1,0:T(4,128)(2,1)S(1)} %collective-permute-done.6), channel_id=1, source_target_pairs={{0,1},{1,2},{2,3},{3,4},{4,5},{5,6},{6,7},{7,8},{8,9},{9,10},{10,1... | collective-permute-start | bytes 221192 | tf_op jit(solution)/shard_map/ppermute | solution.py:19
  56.6 6.7 %collective-permute-start.8 = (bf16[16,3,768]{2,1,0:T(4,128)(2,1)S(1)}, bf16[16,3,768]{2,1,0:T(4,128)(2,1)S(1)}, u32[]{:S(2)}, u32[]{:S(2)}) collective-permute-start(bf16[16,3,768]{2,1,0:T(4,128)(2,1)S(1)} %collective-permute-done.7), channel_id=1, source_target_pairs={{0,1},{1,2},{2,3},{3,4},{4,5},{5,6},{6,7},{7,8},{8,9},{9,10},{10,1... | collective-permute-start | bytes 221192 | tf_op jit(solution)/shard_map/ppermute | solution.py:19
  63.3 6.7 %collective-permute-start.9 = (bf16[16,3,768]{2,1,0:T(4,128)(2,1)S(1)}, bf16[16,3,768]{2,1,0:T(4,128)(2,1)S(1)}, u32[]{:S(2)}, u32[]{:S(2)}) collective-permute-start(bf16[16,3,768]{2,1,0:T(4,128)(2,1)S(1)} %collective-permute-done.8), channel_id=1, source_target_pairs={{0,1},{1,2},{2,3},{3,4},{4,5},{5,6},{6,7},{7,8},{8,9},{9,10},{10,1... | collective-permute-start | bytes 221192 | tf_op jit(solution)/shard_map/ppermute | solution.py:19
  70.1 6.7 %collective-permute-start.10 = (bf16[16,3,768]{2,1,0:T(4,128)(2,1)S(1)}, bf16[16,3,768]{2,1,0:T(4,128)(2,1)S(1)}, u32[]{:S(2)}, u32[]{:S(2)}) collective-permute-start(bf16[16,3,768]{2,1,0:T(4,128)(2,1)S(1)} %collective-permute-done.9), channel_id=1, source_target_pairs={{0,1},{1,2},{2,3},{3,4},{4,5},{5,6},{6,7},{7,8},{8,9},{9,10},{10,1... | collective-permute-start | bytes 221192 | tf_op jit(solution)/shard_map/ppermute | solution.py:19
  76.8 6.7 %collective-permute-start.11 = (bf16[16,3,768]{2,1,0:T(4,128)(2,1)S(1)}, bf16[16,3,768]{2,1,0:T(4,128)(2,1)S(1)}, u32[]{:S(2)}, u32[]{:S(2)}) collective-permute-start(bf16[16,3,768]{2,1,0:T(4,128)(2,1)S(1)} %collective-permute-done.10), channel_id=1, source_target_pairs={{0,1},{1,2},{2,3},{3,4},{4,5},{5,6},{6,7},{7,8},{8,9},{9,10},{10,1... | collective-permute-start | bytes 221192 | tf_op jit(solution)/shard_map/ppermute | solution.py:19
  83.5 6.7 %collective-permute-start.12 = (bf16[16,3,768]{2,1,0:T(4,128)(2,1)S(1)}, bf16[16,3,768]{2,1,0:T(4,128)(2,1)S(1)}, u32[]{:S(2)}, u32[]{:S(2)}) collective-permute-start(bf16[16,3,768]{2,1,0:T(4,128)(2,1)S(1)} %collective-permute-done.11), channel_id=1, source_target_pairs={{0,1},{1,2},{2,3},{3,4},{4,5},{5,6},{6,7},{7,8},{8,9},{9,10},{10,1... | collective-permute-start | bytes 221192 | tf_op jit(solution)/shard_map/ppermute | solution.py:19
  90.3 6.7 %collective-permute-start.13 = (bf16[16,3,768]{2,1,0:T(4,128)(2,1)S(1)}, bf16[16,3,768]{2,1,0:T(4,128)(2,1)S(1)}, u32[]{:S(2)}, u32[]{:S(2)}) collective-permute-start(bf16[16,3,768]{2,1,0:T(4,128)(2,1)S(1)} %collective-permute-done.12), channel_id=1, source_target_pairs={{0,1},{1,2},{2,3},{3,4},{4,5},{5,6},{6,7},{7,8},{8,9},{9,10},{10,1... | collective-permute-start | bytes 221192 | tf_op jit(solution)/shard_map/ppermute | solution.py:19
  97.0 6.7 %collective-permute-start.14 = (bf16[16,3,768]{2,1,0:T(4,128)(2,1)S(1)}, bf16[16,3,768]{2,1,0:T(4,128)(2,1)S(1)}, u32[]{:S(2)}, u32[]{:S(2)}) collective-permute-start(bf16[16,3,768]{2,1,0:T(4,128)(2,1)S(1)} %collective-permute-done.13), channel_id=1, source_target_pairs={{0,1},{1,2},{2,3},{3,4},{4,5},{5,6},{6,7},{7,8},{8,9},{9,10},{10,1... | collective-permute-start | bytes 221192 | tf_op jit(solution)/shard_map/ppermute | solution.py:19
  176.6 301.2 %copy-start.2 = (s32[6,20]{1,0:T(8,128)S(1)}, s32[6,20]{1,0:T(8,128)}, u32[]{:S(2)}) copy-start(s32[6,20]{1,0:T(8,128)} %param.9) | copy-start | bytes 1444
  478.2 30.1 %copy-start.1 = (f32[6,256]{1,0:T(8,128)}, f32[6,256]{1,0:T(8,128)S(1)}, u32[]{:S(2)}) copy-start(f32[6,256]{1,0:T(8,128)S(1)} %fusion.10) | copy-start | bytes 18436
